TPU v7x, 256 devices: a whole 4x4x8 slice. The times are simulated.
256 devices in a mesh: row: 16 (over y, z_lo), col: 16 (over z_hi, x, core).
Axes of the slice: x: 4, y: 4, z: 8 (z_hi: 2, z_lo: 4; z = z_hi * 4 + z_lo), core: 2. Of those that a mesh axis runs over, the one named last changes fastest.
Arguments:
- laplacian: float32 [23040, 23040], P('row', 'col'), may hold values from -1 to 1.12, as said below
- block: float32 [23040, 256], P(('row', 'col')), may hold values from -6 to 6
- bounds: float32 [2], replicated, may hold values from 0.25 to 2.1, as said below
Outputs:
- filtered: float32 [23040, 256], P(('row', 'col'))
- rayleigh: float32 [256, 256], replicated
Inputs may be any that keep to these rules, and one draw needn't show every extreme that they name: laplacian is symmetric; its diagonal entries lie in 0.88 to 1.12 and its other entries have magnitude at most 1.14 / sqrt(23040). bounds[0] lies in 0.25 to 0.40 and bounds[1] in 1.95 to 2.10.
All inputs are finite; a program needn't handle non-finite values.
Results may differ from a plain program's by a relative error of at most 0.00025.
Values sent between devices are 32-bit elements; how exact they have to be, the bound alone decides.
A program may use at most 64 MiB of HBM per device.

v0:
```python
import jax
import jax.numpy as jnp
from jax import lax
from jax.sharding import PartitionSpec as P


def relayout(panel_rows, row_index, col_index, tile_rows, tile_cols):
    offset = col_index * tile_cols - row_index * tile_rows
    zeros_pad = jnp.zeros((tile_cols, panel_rows.shape[1]), jnp.float32)
    padded = jnp.concatenate([zeros_pad, panel_rows, zeros_pad], axis=0)
    start_row = jnp.clip(offset + tile_cols, 0, tile_rows + tile_cols)
    sliced = lax.dynamic_slice_in_dim(padded, start_row, tile_cols, 0)
    target = offset + lax.broadcasted_iota(jnp.int32, (tile_cols, 1), 0)
    inside = (target >= 0) & (target < tile_rows)
    return jnp.where(inside, sliced, 0.0)


def body(laplacian, block, bounds):
    row_index = lax.axis_index("row")
    col_index = lax.axis_index("col")
    tile_rows, tile_cols = laplacian.shape
    lower_bound = bounds[0]
    upper_bound = bounds[1]
    center = (upper_bound + lower_bound) * 0.5
    half_width = (upper_bound - lower_bound) * 0.5
    factor_two = 2.0 / half_width
    global_rows = row_index * tile_rows + lax.broadcasted_iota(jnp.int32, (tile_rows, tile_cols), 0)
    global_cols = col_index * tile_cols + lax.broadcasted_iota(jnp.int32, (tile_rows, tile_cols), 1)
    shifted = laplacian - center * (global_rows == global_cols).astype(jnp.float32)

    def through_columns(panel_rows):
        return lax.dot_general(
            shifted,
            panel_rows,
            (((0,), (0,)), ((), ())),
            precision=lax.Precision.HIGHEST,
            preferred_element_type=jnp.float32,
        )

    def through_rows(panel_cols):
        return jnp.dot(
            shifted, panel_cols, precision=lax.Precision.HIGHEST, preferred_element_type=jnp.float32
        )

    def gather_rows(values):
        return lax.all_gather(values, "col", axis=0, tiled=True)

    def gather_cols(values):
        return lax.all_gather(values, "row", axis=0, tiled=True)

    def column_sum(values):
        return lax.psum_scatter(values, "row", scatter_dimension=0, tiled=True)

    def row_sum(values):
        return lax.psum_scatter(values, "col", scatter_dimension=0, tiled=True)

    filter_one = column_sum(through_columns(gather_rows(block))) / half_width
    filter_two = factor_two * row_sum(through_rows(gather_cols(filter_one))) - block
    filter_three = factor_two * column_sum(through_columns(gather_rows(filter_two))) - filter_one
    filter_four = factor_two * row_sum(through_rows(gather_cols(filter_three))) - filter_two
    panel_four = gather_rows(filter_four)
    dims_inner = (((0,), (0,)), ((), ()))
    image_piece, moved_piece = (
        lax.psum_scatter(through_columns(panel_four), "row", scatter_dimension=0, tiled=True),
        lax.psum_scatter(
            relayout(panel_four, row_index, col_index, tile_rows, tile_cols),
            "row",
            scatter_dimension=0,
            tiled=True,
        ),
    )
    gram_part = lax.dot_general(
        moved_piece,
        moved_piece,
        dims_inner,
        precision=lax.Precision.HIGHEST,
        preferred_element_type=jnp.float32,
    )
    image_part = lax.dot_general(
        moved_piece,
        image_piece,
        dims_inner,
        precision=lax.Precision.HIGHEST,
        preferred_element_type=jnp.float32,
    )
    gram, projected = lax.psum((gram_part, image_part), ("row", "col"))
    projected = projected + center * gram
    projected = (projected + projected.T) * 0.5
    factor = jnp.linalg.cholesky(gram)
    first_solve = jax.scipy.linalg.solve_triangular(factor, projected, lower=True)
    rayleigh = jax.scipy.linalg.solve_triangular(factor, first_solve.T, lower=True)
    return (filter_four, rayleigh)


def solution(mesh):
    placed = (P("row", "col"), P(("row", "col"), None), P())
    return jax.shard_map(
        body, mesh=mesh, in_specs=placed, out_specs=(P(("row", "col"), None), P()), check_vma=False
    )
```

profile of v0, /device:TPU:1, one launch (start us, length us, event | category | flops | bytes accessed | tf_op | source)
XLA Modules:
  0.0 1089.6 jit_solution(2360731310481953332)
XLA Ops:
  10.6 63.4 %all-gather.11.cloned.1.call-done = f32[16,90,256]{2,1,0:T(8,128)} async-done(((f32[1,90,256]{2,1,0:T(8,128)}), f32[16,90,256]{2,1,0:T(8,128)}) %all-gather.11.cloned.1.call-update) | async-done | bytes 1474576 | tf_op jit(solution)/shard_map/all_gather | solution.py:46
  74.0 1.5 reshape.61
  75.5 17.9 %fusion.41 = f32[1440,256]{1,0:T(8,128)S(1)} fusion(f32[1440,256]{1,0:T(8,128)S(1)} %reshape.61, f32[1440,1440]{1,0:T(8,128)} %param.5, f32[]{:T(128)} %bitcast.1, s32[1440]{0:T(1024)S(1)} %get-tuple-element.45, s32[1440]{0:T(1024)S(1)} %get-tuple-element.46), kind=kOutput, calls=%fused_computation.71 | convolution fusion | flops 6376320000 | bytes 11255044 | tf_op jit(solution)/shard_map/dot_general | solution.py:32
  93.4 48.7 %fusion = f32[96,256]{1,0:T(8,128)S(1)} fusion(f32[1440,256]{1,0:T(8,128)S(1)} %fusion.41), kind=kCustom, calls=%all-reduce-scatter | all-reduce-scatter fusion | flops 393217 | bytes 1573888
  142.1 1.7 collective-permute-start
  147.6 75.7 %all-gather.13.cloned.1.call-done = f32[16,90,256]{2,1,0:T(8,128)} async-done(((f32[1,90,256]{2,1,0:T(8,128)}), f32[16,90,256]{2,1,0:T(8,128)}) %all-gather.13.cloned.1.call-update) | async-done | bytes 1474576 | tf_op jit(solution)/shard_map/all_gather | solution.py:49
  223.3 1.5 reshape.63
  224.8 10.1 fusion.40
  234.9 59.2 %fusion.1 = f32[96,256]{1,0:T(8,128)S(1)} fusion(f32[1440,256]{1,0:T(8,128)S(1)} %fusion.40), kind=kCustom, calls=%all-reduce-scatter.1 | all-reduce-scatter fusion | flops 393217 | bytes 1573888
  294.1 2.4 collective-permute-start.1
  297.8 6.1 collective-permute-done.1
  304.9 62.5 %all-gather.15.cloned.1.call-done = f32[16,90,256]{2,1,0:T(8,128)} async-done(((f32[1,90,256]{2,1,0:T(8,128)}), f32[16,90,256]{2,1,0:T(8,128)}) %all-gather.15.cloned.1.call-update) | async-done | bytes 1474576 | tf_op jit(solution)/shard_map/all_gather | solution.py:46
  368.9 17.9 %fusion.39 = f32[1440,256]{1,0:T(8,128)S(1)} fusion(f32[1440,256]{1,0:T(8,128)S(1)} %reshape.65, f32[1440,1440]{1,0:T(8,128)} %param.5, f32[]{:T(128)} %bitcast.1, s32[1440]{0:T(1024)S(1)} %get-tuple-element.45, s32[1440]{0:T(1024)S(1)} %get-tuple-element.46), kind=kOutput, calls=%fused_computation.69 | convolution fusion | flops 6376320000 | bytes 11255044 | tf_op jit(solution)/shard_map/dot_general | solution.py:32
  386.7 48.6 %fusion.2 = f32[96,256]{1,0:T(8,128)S(1)} fusion(f32[1440,256]{1,0:T(8,128)S(1)} %fusion.39), kind=kCustom, calls=%all-reduce-scatter.2 | all-reduce-scatter fusion | flops 393217 | bytes 1573888
  435.4 1.7 collective-permute-start.2
  437.1 1.6 collective-permute-done.2
  439.7 10.4 all-gather.19.cloned.1.call-start
  450.1 66.6 %all-gather.17.cloned.1.call-done = f32[16,90,256]{2,1,0:T(8,128)} async-done(((f32[1,90,256]{2,1,0:T(8,128)}), f32[16,90,256]{2,1,0:T(8,128)}) %all-gather.17.cloned.1.call-update) | async-done | bytes 1474576 | tf_op jit(solution)/shard_map/all_gather | solution.py:49
  518.2 10.1 fusion.38
  528.3 59.1 %fusion.3 = f32[96,256]{1,0:T(8,128)S(1)} fusion(f32[1440,256]{1,0:T(8,128)S(1)} %fusion.38), kind=kCustom, calls=%all-reduce-scatter.3 | all-reduce-scatter fusion | flops 393217 | bytes 1573888
  587.4 2.4 collective-permute-start.3
  589.7 7.4 collective-permute-done.3
  598.1 62.4 %all-gather.19.cloned.1.call-done = f32[16,90,256]{2,1,0:T(8,128)} async-done(((f32[1,90,256]{2,1,0:T(8,128)}), f32[16,90,256]{2,1,0:T(8,128)}) %all-gather.19.cloned.1.call-update) | async-done | bytes 1474576 | tf_op jit(solution)/shard_map/all_gather | solution.py:46
  662.1 19.0 %fusion.37 = f32[1440,256]{1,0:T(8,128)} fusion(f32[1440,256]{1,0:T(8,128)S(1)} %reshape.69, f32[1440,1440]{1,0:T(8,128)} %param.5, f32[]{:T(128)} %bitcast.1, s32[1440]{0:T(1024)S(1)} %get-tuple-element.45, s32[1440]{0:T(1024)S(1)} %get-tuple-element.46), kind=kOutput, calls=%fused_computation.67 | convolution fusion | flops 6376320000 | bytes 11255044 | tf_op jit(solution)/shard_map/dot_general | solution.py:32
  682.0 71.7 %fusion.42 = (f32[96,256]{1,0:T(8,128)S(1)}, f32[96,256]{1,0:T(8,128)S(1)}) fusion(f32[1440,256]{1,0:T(8,128)} %fusion.37, f32[1440,256]{1,0:T(8,128)S(1)} %fusion.8), kind=kCustom, calls=%all-reduce-scatter.6 | all-reduce-scatter fusion | flops 786433 | bytes 3146752
  755.0 1.5 collective-permute-start.5
  759.5 257.1 %all-reduce.17.cloned.1.call-done = (f32[256,256]{0,1:T(8,128)}, f32[256,256]{0,1:T(8,128)}) async-done(((f32[256,256]{0,1:T(8,128)}, f32[256,256]{0,1:T(8,128)}), (f32[256,256]{0,1:T(8,128)}, f32[256,256]{0,1:T(8,128)})) %all-reduce.17.cloned.1.call-update) | async-done | bytes 524304 | tf_op jit(solution)/shard_map/psum | solution.py:86
  1018.9 11.7 %cholesky.50 = f32[128,128]{1,0:T(8,128)S(1)} custom-call(f32[128,128]{1,0:T(8,128)S(1)} %cholesky.118), custom_call_target="Cholesky" | custom-call | tf_op jit(solution)/shard_map/jit(cholesky)/cholesky | solution.py:89
  1030.7 9.8 custom-call.14
  1041.0 11.7 %cholesky.105 = f32[128,128]{1,0:T(8,128)S(1)} custom-call(f32[128,128]{1,0:T(8,128)S(1)} %convolution_subtract_fusion.2), custom_call_target="Cholesky" | custom-call | tf_op jit(solution)/shard_map/jit(cholesky)/cholesky | solution.py:89
  1055.5 4.1 while.4
  1059.6 19.9 %custom-call.17 = f32[2,128,128]{1,2,0:T(8,128)S(1)} custom-call(f32[2,128,128]{2,1,0:T(8,128)S(1)} %get-tuple-element.18), custom_call_target="InvertDiagBlocksLowerTriangular" | custom-call | tf_op jit(solution)/shard_map/jit(_solve_triangular)/triangular_solve | solution.py:91
  (81 shorter events, 28.2 us)
Async XLA Ops:
  7.2 66.8 %all-gather.11.cloned.1.call-start = ((), (), s32[]{:S(2)}) async-start(), calls=%async_computation | async-start | bytes 1671168 | tf_op jit(solution)/shard_map/all_gather | solution.py:46
  7.9 215.4 %all-gather.13.cloned.1.call-start = ((), (), s32[]{:S(2)}) async-start(), calls=%async_computation.1 | async-start | bytes 1671168 | tf_op jit(solution)/shard_map/all_gather | solution.py:49
  93.4 51.8 %copy-start.2 = (u32[256]{0:T(256)S(1)}, u32[256]{0:T(256)}, u32[]{:S(2)}) copy-start(u32[256]{0:T(256)} %constant.130) | copy-start | bytes 3076
  142.1 4.2 collective-permute-start
  147.3 220.1 %all-gather.15.cloned.1.call-start = ((), (), s32[]{:S(2)}) async-start(), calls=%async_computation.2 | async-start | bytes 1671168 | tf_op jit(solution)/shard_map/all_gather | solution.py:46
  234.9 61.7 %copy-start.1 = (u32[256]{0:T(256)S(1)}, u32[256]{0:T(256)}, u32[]{:S(2)}) copy-start(u32[256]{0:T(256)} %constant.134) | copy-start | bytes 3076
  234.9 69.3 %copy-start = (f32[90,256]{1,0:T(8,128)S(1)}, f32[90,256]{1,0:T(8,128)}, u32[]{:S(2)}) copy-start(f32[90,256]{1,0:T(8,128)} %param.6) | copy-start | bytes 276484
  294.1 9.7 collective-permute-start.1
  304.8 211.9 %all-gather.17.cloned.1.call-start = ((), (), s32[]{:S(2)}) async-start(), calls=%async_computation.3 | async-start | bytes 1671168 | tf_op jit(solution)/shard_map/all_gather | solution.py:49
  435.4 3.3 collective-permute-start.2
  439.7 220.9 %all-gather.19.cloned.1.call-start = ((), (), s32[]{:S(2)}) async-start(), calls=%async_computation.4 | async-start | bytes 1671168 | tf_op jit(solution)/shard_map/all_gather | solution.py:46
  587.4 9.7 collective-permute-start.3
  598.1 418.5 %all-reduce.17.cloned.1.call-start = ((), (), s32[]{:S(2)}) async-start(), calls=%async_computation.5 | async-start | bytes 1048576 | tf_op jit(solution)/shard_map/psum | solution.py:86
  753.7 2.9 collective-permute-start.4
  755.0 3.0 collective-permute-start.5
Sparse Core Ops, SparseCore 0:
  10.7 63.2 all-gather.10
  147.4 75.8 all-gather.12
  305.0 62.3 all-gather.14
  439.8 76.8 all-gather.16
  598.2 62.3 all-gather.18
  759.6 256.9 all-reduce.16
where the time goes:
time: 1100 us; the launch traced here: 1090 us
  waiting for transfers between devices  604 us (55%)
  blocking collectives  287 us (26%)
  matrix products  79.5 us (7%)
  other arithmetic  60 us (5%)
  starting transfers between devices  21.7 us (2%)
  between operations  20.4 us (2%)
  local copies, waits for them, and re-layouts  17.1 us (2%)
    unnamed x5, blocking collectives  287 us
    psum x1, waiting for transfers between devices, body(): gram, projected = lax.psum((gram_part, image_part), ('row', 'col'))  257 us
    all_gather x3, waiting for transfers between devices, gather_rows(): return lax.all_gather(values, 'col', axis=0, tiled=True)  188 us
    all_gather x2, waiting for transfers between devices, gather_cols(): return lax.all_gather(values, 'row', axis=0, tiled=True)  142 us
    dot_general x3, matrix products, through_columns(): lax.dot_general(shifted, panel_rows, (((0,), (0,)), ((), ())), precision=...  54.7 us
    another operation x7, other arithmetic, body(): factor = jnp.linalg.cholesky(gram)  34.6 us
  transfers between devices with their start and end apart: 12, of which 10 were waited for; matrix products, arithmetic and copies ran while one was open for 0% of the time, Pallas kernels for 0%

commit v1 on v0

v1 whole, which is shorter than its diff:
```python
import functools

import jax
import jax.numpy as jnp
from jax import lax
from jax.experimental import pallas as pl
from jax.experimental.pallas import tpu as pltpu
from jax.sharding import PartitionSpec as P

MESH = pl.DeviceIdType.MESH
F32 = jnp.float32
BF16 = jnp.bfloat16
L = 128
TILE = 1440
PAD = 1536
PIECE = 96
OWN = 90
LEAD = 0

CHAIN = dict(
    raw0=((2, 4, 2, PIECE, L), F32),
    panel0=((PAD, L), F32),
    panel_r=((2, 4, 2, PIECE, L), F32),
    panel_c=((4, 4, 2, 48, L), F32),
    panel_f=((4, 4, 2, 48, L), F32),
    part_c=((4, 4, 2, 48, L), F32),
    part_r=((2, 4, 2, PIECE, L), F32),
    vcat=((PAD, 2 * L), BF16),
    core_in=((4, 2, PIECE, L), F32),
    y_in=((6, 2, 2, 48, L), F32),
    y_sum=((4, 2, 48, L), F32),
    z_in=((6, 48, L), F32),
    x_in=((6, PIECE, L), F32),
    x_sum=((2, PIECE, L), F32),
    h_in=((PIECE, L), F32),
    z1=((2, 48, L), F32),
    z2=((PIECE, L), F32),
    z4=((2, 48, L), F32),
)
REDUCE = dict(
    a=((2, 4, 4, 8, 256), F32),
    total=((2, 4, 4, 8, 256), F32),
    core_in=((4, 4, 8, 256), F32),
    x_in=((3, 4, 8, 256), F32),
    y_in=((3, 8, 256), F32),
    z_in=((4, 8, 256), F32),
    h_own=((8, 256), F32),
    h_in=((8, 256), F32),
)
SHARED = dict(
    stage=((TILE, TILE), F32),
    strip=((128, PAD), F32),
    mat_h=((PAD, PAD), BF16),
    mat_l=((PAD, PAD), BF16),
    tra_h=((PAD, PAD), BF16),
    tra_l=((PAD, PAD), BF16),
    own4=((128, 256), F32),
    ft_h=((256, PAD), BF16),
    ft_l=((256, PAD), BF16),
    img_h=((PAD, 256), BF16),
    img_l=((PAD, 256), BF16),
)
AT_START, AT_ROW, AT_ROWG, AT_COL, AT_COLG, AT_TURN, AT_LAST, CHAIN_SEMS = 0, 11, 23, 33, 42, 53, 54, 64
REDUCE_SEMS = 18


def split(value):
    high = value.astype(BF16)
    return high, (value - high.astype(F32)).astype(BF16)


def run(tasks):
    tasks = list(tasks)
    while tasks:
        tasks = [t for t in tasks if next(t, "end") != "end"]


class Kernel:
    def __init__(self):
        r, c = lax.axis_index("row"), lax.axis_index("col")
        self.r, self.c = r, c
        self.y, self.z = r // 4, r % 4
        self.zh, self.x, self.core = c // 8, (c // 2) % 4, c % 2
        self.pos = self.core * 8 + self.x * 2 + self.zh

    def yn(self, d):
        return ((self.y + d) % 4) * 4 + self.z, self.c

    def zn(self, d):
        return self.y * 4 + (self.z + d) % 4, self.c

    def xn(self, d):
        return self.r, self.zh * 8 + ((self.x + d) % 4) * 2 + self.core

    def hn(self):
        return self.r, (1 - self.zh) * 8 + self.x * 2 + self.core

    def cn(self):
        return self.r, self.zh * 8 + self.x * 2 + 1 - self.core

    def turn_to(self):
        return self.pos, self.r

    def turn_from(self):
        r = self.r
        return self.c, (r % 2) * 8 + ((r // 2) % 4) * 2 + r // 8


class Link:
    def __init__(self, send, recv):
        self.send, self.recv, self.open = send, recv, []

    def put(self, src, dst, k, device):
        copy = pltpu.make_async_remote_copy(
            src_ref=src, dst_ref=dst, send_sem=self.send.at[k], recv_sem=self.recv.at[k], device_id=device, device_id_type=MESH
        )
        copy.start()
        self.open.append(copy)

    def got(self, dst, k, device):
        pltpu.make_async_remote_copy(
            src_ref=dst, dst_ref=dst, send_sem=self.send.at[k], recv_sem=self.recv.at[k], device_id=device, device_id_type=MESH
        ).wait_recv()

    def flush(self):
        for copy in self.open:
            copy.wait_send()
        self.open = []


def ring_sum(link, k, i, near, half, box, out, ready):
    a, b, d = (i + 1) % 4, (i + 3) % 4, (i + 2) % 4
    ready(d)
    link.put(half(d, 0), box.at[0], k, near(1))
    link.put(half(d, 1), box.at[1], k + 1, near(3))
    ready(a)
    link.put(half(a, 1), box.at[2], k + 2, near(1))
    ready(b)
    link.put(half(b, 0), box.at[3], k + 3, near(3))
    ready(i)
    yield
    link.got(box.at[0], k, near(3))
    half(a, 0)[...] += box[0]
    link.put(half(a, 0), box.at[4], k + 4, near(1))
    link.got(box.at[1], k + 1, near(1))
    half(b, 1)[...] += box[1]
    link.put(half(b, 1), box.at[5], k + 5, near(3))
    yield
    link.got(box.at[2], k + 2, near(3))
    link.got(box.at[3], k + 3, near(1))
    link.got(box.at[4], k + 4, near(3))
    link.got(box.at[5], k + 5, near(1))
    out(0, half(i, 0)[...] + box[4] + box[3])
    out(1, half(i, 1)[...] + box[2] + box[5])


def nothing(j):
    pass


def gather_col(me, link, k, panel):
    core, x, zh = me.core, me.x, me.zh
    a, b, d = (x + 1) % 4, (x + 3) % 4, (x + 2) % 4

    def put(ref, j, device):
        link.put(ref, ref, k + j, device)

    put(panel.at[core, x, zh], 0, me.hn())
    put(panel.at[core, x, zh], 1, me.xn(1))
    put(panel.at[core, x, zh], 2, me.xn(3))
    yield
    link.got(panel.at[core, x, 1 - zh], k, me.hn())
    put(panel.at[core, x, 1 - zh], 3, me.xn(1))
    put(panel.at[core, x, 1 - zh], 4, me.xn(3))
    put(panel.at[core, x], 7, me.cn())
    yield
    link.got(panel.at[core, b, zh], k + 1, me.xn(3))
    link.got(panel.at[core, b, 1 - zh], k + 3, me.xn(3))
    put(panel.at[core, b, 0], 5, me.xn(1))
    put(panel.at[core, b], 8, me.cn())
    link.got(panel.at[core, a, zh], k + 2, me.xn(1))
    link.got(panel.at[core, a, 1 - zh], k + 4, me.xn(1))
    put(panel.at[core, a, 1], 6, me.xn(3))
    put(panel.at[core, a], 9, me.cn())
    yield
    link.got(panel.at[core, d, 0], k + 5, me.xn(3))
    link.got(panel.at[core, d, 1], k + 6, me.xn(1))
    put(panel.at[core, d], 10, me.cn())
    yield
    other = 1 - core
    link.got(panel.at[other, x], k + 7, me.cn())
    link.got(panel.at[other, b], k + 8, me.cn())
    link.got(panel.at[other, a], k + 9, me.cn())
    link.got(panel.at[other, d], k + 10, me.cn())


def gather_row(me, link, k, panel):
    y, z = me.y, me.z
    za, zb, zd = (z + 1) % 4, (z + 3) % 4, (z + 2) % 4
    ya, yb, yd = (y + 1) % 4, (y + 3) % 4, (y + 2) % 4

    def put(ref, j, device):
        link.put(ref, ref, k + j, device)

    put(panel.at[y, z], 0, me.zn(1))
    put(panel.at[y, z], 1, me.zn(3))
    yield
    link.got(panel.at[y, zb], k, me.zn(3))
    put(panel.at[y, zb, 0], 2, me.zn(1))
    link.got(panel.at[y, za], k + 1, me.zn(1))
    put(panel.at[y, za, 1], 3, me.zn(3))
    yield
    link.got(panel.at[y, zd, 0], k + 2, me.zn(3))
    link.got(panel.at[y, zd, 1], k + 3, me.zn(1))
    low, high = pl.ds(0, 2), pl.ds(2, 2)
    put(panel.at[y, low], 4, me.yn(1))
    put(panel.at[y, high], 5, me.yn(3))
    put(panel.at[y, high], 6, me.yn(1))
    put(panel.at[y, low], 7, me.yn(3))
    yield
    link.got(panel.at[yb, low], k + 4, me.yn(3))
    put(panel.at[yb, low], 8, me.yn(1))
    link.got(panel.at[ya, high], k + 5, me.yn(1))
    put(panel.at[ya, high], 9, me.yn(3))
    yield
    link.got(panel.at[yb, high], k + 6, me.yn(3))
    link.got(panel.at[ya, low], k + 7, me.yn(1))
    link.got(panel.at[yd, low], k + 8, me.yn(3))
    link.got(panel.at[yd, high], k + 9, me.yn(1))


def split_row_panel(panel, vcat):
    @pl.loop(0, 8)
    def _(i):
        high, low = split(panel[i // 4, i % 4].reshape(2 * PIECE, L))
        rows = pl.ds(pl.multiple_of(i * 192, 192), 192)
        vcat[rows, :L] = high
        vcat[rows, L:] = low


def split_col_panel(panel, vcat):
    @pl.loop(0, 4)
    def _(i):
        high, low = split(panel[i].reshape(384, L))
        rows = pl.ds(pl.multiple_of(i * 384, 384), 384)
        vcat[rows, :L] = high
        vcat[rows, L:] = low


def product(high, low, vcat, chunk):
    rows = pl.ds(pl.multiple_of(chunk * 384, 384), 384)
    wide = jnp.dot(high[rows, :], vcat[...], preferred_element_type=F32)
    rest = jnp.dot(low[rows, :], vcat[:, :L], preferred_element_type=F32)
    return wide[:, :L] + (wide[:, L:] + rest)


def odd_step(me, link, s, b, scale, previous, save):
    split_row_panel(b["panel_r"], b["vcat"]) if previous is not None else None
    part, y_sum, panel = b["part_c"], b["y_sum"], b["panel_c"]
    y, z = me.y, me.z

    def ready(j):
        part[j] = product(s["tra_h"], s["tra_l"], b["vcat"], j).reshape(4, 2, 48, L)

    def out_y(h, value):
        y_sum[pl.ds(2 * h, 2)] = value

    def out_z(h, value):
        value = value * scale
        if previous is not None:
            value = value - previous[h]
        panel[y, z, h] = value
        if save is not None:
            save[h] = value

    yield from ring_sum(link, AT_ROW, y, me.yn, lambda j, h: part.at[j, pl.ds(2 * h, 2)], b["y_in"], out_y, ready)
    yield from ring_sum(link, AT_ROW + 6, z, me.zn, lambda j, h: y_sum.at[j, h], b["z_in"], out_z, nothing)
    yield from gather_row(me, link, AT_ROWG, panel)
    link.flush()


def even_sum(me, link, s, b, scale, previous, store):
    split_col_panel(b["panel_c"], b["vcat"])
    part, box = b["part_r"], b["core_in"]
    core, x, zh = me.core, me.x, me.zh
    other, first = 1 - core, 1 - x // 2
    k = AT_COL

    def compute(half, pair):
        value = product(s["mat_h"], s["mat_l"], b["vcat"], half * 2 + pair)
        part[half, pl.ds(2 * pair, 2)] = value.reshape(2, 2, PIECE, L)

    compute(other, first)
    link.put(part.at[other, pl.ds(2 * first, 2)], box.at[pl.ds(2 * first, 2)], k, me.cn())
    last = 1 - first
    compute(other, last)
    link.put(part.at[other, pl.ds(2 * last, 2)], box.at[pl.ds(2 * last, 2)], k + 1, me.cn())
    compute(core, first)
    compute(core, last)
    yield
    turn = []

    def ready(j):
        if len(turn) == 0:
            link.got(box.at[pl.ds(2 * first, 2)], k, me.cn())
        if len(turn) == 1:
            link.got(box.at[pl.ds(2 * last, 2)], k + 1, me.cn())
        turn.append(j)
        part[core, j] += box[j]

    x_sum = b["x_sum"]

    def out_x(h, value):
        x_sum[h] = value

    yield from ring_sum(link, k + 2, x, me.xn, lambda j, h: part.at[core, j, h], b["x_in"], out_x, ready)
    link.put(x_sum.at[1 - zh], b["h_in"], k + 8, me.hn())
    yield
    link.got(b["h_in"], k + 8, me.hn())
    store((x_sum[zh] + b["h_in"][...]) * scale - previous())


def chain(me, link, s, b, half_width, first):
    def scaled(n):
        return n / half_width

    yield from gather_col(me, link, AT_START, b["raw0"])
    panel0 = b["panel0"]
    panel0[TILE:, :] = jnp.zeros((PAD - TILE, L), F32)
    for c in range(16):
        panel0[c * OWN : (c + 1) * OWN, :] = b["raw0"][c % 2, (c // 2) % 4, c // 8, :OWN, :]

    @pl.loop(0, 4)
    def _(i):
        rows = pl.ds(pl.multiple_of(i * 384, 384), 384)
        high, low = split(panel0[rows, :])
        b["vcat"][rows, :L] = high
        b["vcat"][rows, L:] = low

    if first is not None:
        first()
    link.flush()
    yield from odd_step(me, link, s, b, scaled(1.0), None, b["z1"])
    z2, panel_r = b["z2"], b["panel_r"]

    def store2(value):
        z2[...] = value
        panel_r[me.core, me.x, me.zh] = value

    rows = pl.ds(pl.multiple_of(me.pos * PIECE, PIECE), PIECE)
    yield from even_sum(me, link, s, b, scaled(2.0), lambda: panel0[rows, :], store2)
    yield from gather_col(me, link, AT_COLG, panel_r)
    link.flush()
    yield from odd_step(me, link, s, b, scaled(2.0), b["z1"], None)

    def store4(value):
        panel_r[me.core, me.x, me.zh] = value
        b["z4"][...] = value.reshape(2, 48, L)

    yield from even_sum(me, link, s, b, scaled(2.0), lambda: z2[...], store4)
    link.flush()


def turned_gather(me, link, b, alone):
    panel, z4 = b["panel_f"], b["z4"]
    row, col = me.turn_to()
    slot = panel.at[row // 4, row % 4]

    def copy():
        return pltpu.make_async_remote_copy(
            src_ref=z4,
            dst_ref=slot,
            send_sem=link.send.at[AT_TURN],
            recv_sem=link.recv.at[AT_TURN],
            device_id=(row, col),
            device_id_type=MESH,
        )

    @pl.when(jnp.logical_not(alone))
    def _():
        copy().start()

    @pl.when(alone)
    def _():
        panel[me.y, me.z] = z4[...]

    yield

    @pl.when(jnp.logical_not(alone))
    def _():
        link.got(panel.at[me.y, me.z], AT_TURN, me.turn_from())
        copy().wait_send()

    yield from gather_row(me, link, AT_LAST, panel)


def all_sum(me, link, b):
    a, total = b["a"], b["total"]
    y, z, zh, x, core = me.y, me.z, me.zh, me.x, me.core
    other = 1 - core
    link.put(a.at[other], b["core_in"], 0, me.cn())
    yield
    link.got(b["core_in"], 0, me.cn())
    a[core] += b["core_in"][...]
    for d in (1, 2, 3):
        link.put(a.at[core, (x + d) % 4], b["x_in"].at[d - 1], d, me.xn(d))
    yield
    for d in (1, 2, 3):
        link.got(b["x_in"].at[d - 1], d, me.xn(4 - d))
    a[core, x] += (b["x_in"][0] + b["x_in"][1]) + b["x_in"][2]
    for d in (1, 2, 3):
        link.put(a.at[core, x, (y + d) % 4], b["y_in"].at[d - 1], 3 + d, me.yn(d))
    yield
    for d in (1, 2, 3):
        link.got(b["y_in"].at[d - 1], 3 + d, me.yn(4 - d))
    own = a[core, x, y] + ((b["y_in"][0] + b["y_in"][1]) + b["y_in"][2])
    b["z_in"][z] = own
    for d in (1, 2, 3):
        link.put(b["z_in"].at[z], b["z_in"].at[z], 6 + d, me.zn(d))
    yield
    for d in (1, 2, 3):
        link.got(b["z_in"].at[(z + 4 - d) % 4], 6 + d, me.zn(4 - d))
    b["h_own"][...] = (b["z_in"][0] + b["z_in"][1]) + (b["z_in"][2] + b["z_in"][3])
    link.put(b["h_own"], b["h_in"], 10, me.hn())
    yield
    link.got(b["h_in"], 10, me.hn())
    link.flush()
    total[core, x, y] = b["h_own"][...] + b["h_in"][...]
    for d in (1, 2, 3):
        link.put(total.at[core, x, y], total.at[core, x, y], 10 + d, me.yn(d))
    yield
    for d in (1, 2, 3):
        link.got(total.at[core, x, (y + 4 - d) % 4], 10 + d, me.yn(4 - d))
    for d in (1, 2, 3):
        link.put(total.at[core, x], total.at[core, x], 13 + d, me.xn(d))
    yield
    for d in (1, 2, 3):
        link.got(total.at[core, (x + 4 - d) % 4], 13 + d, me.xn(4 - d))
    link.put(total.at[core], total.at[core], 17, me.cn())
    yield
    link.got(total.at[other], 17, me.cn())
    link.flush()


def body_kernel(lap, block, bounds, filtered, gram, projected, *scratch):
    names = list(SHARED), list(CHAIN), list(CHAIN), list(REDUCE), list(REDUCE)
    groups, at = [], 0
    for group in names:
        groups.append(dict(zip(group, scratch[at : at + len(group)])))
        at += len(group)
    s, *chains, red_g, red_p = groups
    lap_sem, *sems = scratch[at:]
    links = [Link(sems[2 * i], sems[2 * i + 1]) for i in range(4)]
    me = Kernel()
    to_row, to_col = me.turn_to()
    alone = jnp.logical_and(to_row == me.r, to_col == me.c)

    load = pltpu.make_async_copy(lap, s["stage"], lap_sem)
    load.start()
    for h, b in enumerate(chains):
        own = b["raw0"].at[me.core, me.x, me.zh]
        own[OWN - 2 :, :] = jnp.zeros((PIECE - OWN + 2, L), F32)
        own[:OWN, :] = block[:, h * L : (h + 1) * L]

    barrier = pltpu.get_barrier_semaphore()
    near = [f(d) for f in (me.yn, me.zn, me.xn) for d in (1, 2, 3)] + [me.hn(), me.cn()]
    for device in near:
        pl.semaphore_signal(barrier, inc=1, device_id=device, device_id_type=MESH)

    @pl.when(jnp.logical_not(alone))
    def _():
        pl.semaphore_signal(barrier, inc=1, device_id=me.turn_to(), device_id_type=MESH)
        pl.semaphore_signal(barrier, inc=1, device_id=me.turn_from(), device_id_type=MESH)

    pl.semaphore_wait(barrier, jnp.where(alone, len(near), len(near) + 2))

    center = (bounds[1] + bounds[0]) * 0.5
    half_width = (bounds[1] - bounds[0]) * 0.5

    def prepare():
        load.wait()
        shift = jnp.where(me.r == me.c, center, 0.0)
        strip = s["strip"]
        strip[...] = jnp.zeros_like(strip)

        def strip_of(start, count):
            value = s["stage"][pl.ds(start, count), :]
            row = start + lax.broadcasted_iota(jnp.int32, (count, TILE), 0)
            col = lax.broadcasted_iota(jnp.int32, (count, TILE), 1)
            strip[:count, :TILE] = value - jnp.where(row == col, shift, 0.0)

        def spread(start):
            whole = strip[...]
            high, low = split(whole)
            s["mat_h"][pl.ds(start, 128), :] = high
            s["mat_l"][pl.ds(start, 128), :] = low
            high, low = split(whole.T)
            s["tra_h"][:, pl.ds(start, 128)] = high
            s["tra_l"][:, pl.ds(start, 128)] = low

        @pl.loop(0, TILE // 128)
        def _(i):
            start = pl.multiple_of(i * 128, 128)
            strip_of(start, 128)
            spread(start)

        strip[...] = jnp.zeros_like(strip)
        strip_of(TILE // 128 * 128, TILE % 128)
        spread(TILE // 128 * 128)

    one = chain(me, links[0], s, chains[0], half_width, prepare)
    two = chain(me, links[1], s, chains[1], half_width, None)
    next(one)
    next(two)
    for _ in range(LEAD):
        next(one)
    run([one, two])

    own4 = s["own4"]
    own4[PIECE:, :] = jnp.zeros((128 - PIECE, 256), F32)
    for h, b in enumerate(chains):
        own4[:PIECE, h * L : (h + 1) * L] = b["z4"][...].reshape(PIECE, L)
    high, low = split(own4[...])
    dims = (((0,), (0,)), ((), ()))

    def pair(p, q):
        return lax.dot_general(p, q, dims, preferred_element_type=F32)

    part = pair(high, high) + (pair(high, low) + pair(low, high))
    red_g["a"][...] = part.reshape(2, 4, 4, 8, 256)
    run(
        [gather_col(me, links[h], AT_COLG, chains[h]["panel_r"]) for h in (0, 1)]
        + [turned_gather(me, links[h], chains[h], alone) for h in (0, 1)]
        + [all_sum(me, links[2], red_g)]
    )
    for link in links[:2]:
        link.flush()
    for c in range(16):

        @pl.when(me.c == c)
        def _(c=c):
            for h, b in enumerate(chains):
                row = 0
                while row < OWN:
                    at = c * OWN + row
                    p, inside = at // PIECE, at % PIECE
                    count = min(PIECE - inside, OWN - row)
                    filtered[row : row + count, h * L : (h + 1) * L] = b["panel_r"][p // 8, (p // 2) % 4, p % 2, inside : inside + count, :]
                    row += count

    for h, b in enumerate(chains):
        split_row_panel(b["panel_r"], b["vcat"])

        @pl.loop(0, 4)
        def _(j, b=b, h=h):
            rows = pl.ds(pl.multiple_of(j * 384, 384), 384)
            high, low = split(product(s["tra_h"], s["tra_l"], b["vcat"], j))
            s["img_h"][rows, h * L : (h + 1) * L] = high
            s["img_l"][rows, h * L : (h + 1) * L] = low
            high, low = split(b["panel_f"][j].reshape(384, L).T)
            s["ft_h"][h * L : (h + 1) * L, rows] = high
            s["ft_l"][h * L : (h + 1) * L, rows] = low

    def inner(p, q):
        return jnp.dot(p[...], q[...], preferred_element_type=F32)

    part = inner(s["ft_h"], s["img_h"]) + (inner(s["ft_h"], s["img_l"]) + inner(s["ft_l"], s["img_h"]))
    red_p["a"][...] = part.reshape(2, 4, 4, 8, 256)
    run([all_sum(me, links[3], red_p)])
    gram[...] = red_g["total"][...].reshape(256, 256)
    projected[...] = red_p["total"][...].reshape(256, 256)


def body(laplacian, block, bounds):
    vmem = pl.BlockSpec(memory_space=pltpu.VMEM)
    scratch = [pltpu.VMEM(shape, kind) for group in (SHARED, CHAIN, CHAIN, REDUCE, REDUCE) for shape, kind in group.values()]
    scratch.append(pltpu.SemaphoreType.DMA)
    for count in (CHAIN_SEMS, CHAIN_SEMS, REDUCE_SEMS, REDUCE_SEMS):
        scratch += [pltpu.SemaphoreType.DMA((count,)), pltpu.SemaphoreType.DMA((count,))]
    square = jax.ShapeDtypeStruct((256, 256), F32)
    filtered, gram, projected = pl.pallas_call(
        body_kernel,
        out_shape=(jax.ShapeDtypeStruct(block.shape, F32), square, square),
        in_specs=[pl.BlockSpec(memory_space=pl.ANY), vmem, pl.BlockSpec(memory_space=pltpu.SMEM)],
        out_specs=(vmem, vmem, vmem),
        scratch_shapes=scratch,
        compiler_params=pltpu.CompilerParams(collective_id=0, has_side_effects=True, vmem_limit_bytes=62 * 1024 * 1024),
        name="filter",
    )(laplacian, block, bounds)
    center = (bounds[1] + bounds[0]) * 0.5
    projected = projected + center * gram
    projected = (projected + projected.T) * 0.5
    factor = jnp.linalg.cholesky(gram)
    first_solve = jax.scipy.linalg.solve_triangular(factor, projected, lower=True)
    rayleigh = jax.scipy.linalg.solve_triangular(factor, first_solve.T, lower=True)
    return filtered, rayleigh


def solution(mesh):
    placed = (P("row", "col"), P(("row", "col"), None), P())
    return jax.shard_map(
        body, mesh=mesh, in_specs=placed, out_specs=(P(("row", "col"), None), P()), check_vma=False
    )
```

time: 1100 us -> 319 us (0.29)
  waiting for transfers between devices: 604 us -> 0 us
  blocking collectives: 287 us -> 0 us
  Pallas kernels: 0 us -> 250 us
  matrix products: 79.5 us -> 2.36 us
  starting transfers between devices: 21.7 us -> 0 us
  between operations: 20.4 us -> 3.47 us
    all_gather x5 -> x0, waiting for transfers between devices: 331 us -> none  [the longest x3 188 us: gather_rows(): return lax.all_gather(values, 'col', axis=0, tiled=True)]
    unnamed x5 -> x0, blocking collectives: 287 us -> none
    psum x1 -> x0, waiting for transfers between devices: 257 us -> none  [body(): gram, projected = lax.psum((gram_part, image_part), ('row', 'col'))]
    pallas_call x0 -> x1, Pallas kernels: none -> 250 us  [body(): pl.pallas_call(body_kernel, out_shape=(jax.ShapeDtypeStruct(block.shape,...]
    dot_general x7 -> x0, matrix products: 77.1 us -> none  [the longest x3 54.7 us: through_columns(): lax.dot_general(shifted, panel_rows, (((0,), (0,)), ((), ())), precision=...]
    unnamed x12 -> x0, waiting for transfers between devices: 15.9 us -> none
    another operation x7 -> x6, other arithmetic: 34.6 us -> 34 us  [body(): factor = jnp.linalg.cholesky(gram)]
  transfers between devices with their start and end apart: 12 -> 0, of which waited for: 10 -> 0; matrix products, arithmetic and copies ran while one was open for 0% -> 0% of each run, Pallas kernels for 0% -> 0%
where the time goes in v1:
time: 319 us
  Pallas kernels  250 us (78%)
  other arithmetic  55.8 us (17%)
  local copies, waits for them, and re-layouts  7.7 us (2%)
  between operations  3.47 us (1%)
    pallas_call x1, Pallas kernels, body(): pl.pallas_call(body_kernel, out_shape=(jax.ShapeDtypeStruct(block.shape,...  250 us
    another operation x6, other arithmetic, body(): factor = jnp.linalg.cholesky(gram)  34 us
    another operation x5, other arithmetic, body(): jax.scipy.linalg.solve_triangular(factor, first_solve.T, lower=True)  20.7 us

profile of v1, /device:TPU:1, one launch (start us, length us, event | category | flops | bytes accessed | tf_op | source)
XLA Modules:
  0.0 319.0 jit_solution(2474513377937388906)
XLA Ops:
  0.6 0.0 copy-start.1
  0.6 249.6 %filter.1 = (f32[90,256]{1,0:T(8,128)}, f32[256,256]{1,0:T(8,128)}, f32[256,256]{1,0:T(8,128)}) custom-call(f32[1440,1440]{1,0:T(8,128)} %lap.1, f32[90,256]{1,0:T(8,128)} %block.1, f32[2]{0:T(128)} %bounds.1), custom_call_target="tpu_custom_call" | custom-call | tf_op jit(solution)/shard_map/filter/pallas_call | solution.py:581
  250.2 0.0 copy-start
  250.3 1.1 copy.7
  251.4 1.1 copy.5
  252.5 0.0 copy-done.1
  252.5 0.6 fusion.14
  254.4 0.1 copy.8
  254.6 1.0 fusion.1
  255.6 11.7 %cholesky.50 = f32[128,128]{1,0:T(8,128)S(1)} custom-call(f32[128,128]{1,0:T(8,128)S(1)} %cholesky.118), custom_call_target="Cholesky" | custom-call | tf_op jit(solution)/shard_map/jit(cholesky)/cholesky | solution.py:593
  267.4 9.8 %custom-call.14 = f32[1,128,128]{1,2,0:T(8,128)S(1)} custom-call(f32[1,128,128]{2,1,0:T(8,128)S(1)} %get-tuple-element.38), custom_call_target="InvertDiagBlocksLowerTriangular" | custom-call | tf_op jit(solution)/shard_map/jit(cholesky)/cholesky | solution.py:593
  277.2 0.2 constant_dynamic-update-slice_fusion.1
  277.4 0.3 convolution_subtract_fusion.2
  277.6 11.7 %cholesky.105 = f32[128,128]{1,0:T(8,128)S(1)} custom-call(f32[128,128]{1,0:T(8,128)S(1)} %convolution_subtract_fusion.2), custom_call_target="Cholesky" | custom-call | tf_op jit(solution)/shard_map/jit(cholesky)/cholesky | solution.py:593
  289.4 0.7 compare_reduce_fusion
  291.5 0.3 select_select_fusion
  291.8 0.1 triangular_solve.96
  291.8 4.1 %while.4 = (s32[]{:T(128)}, f32[256,256]{1,0:T(8,128)S(1)}, s32[2,2]{1,0:T(2,128)S(1)}, f32[2,128,128]{2,1,0:T(8,128)S(1)}, s32[]{:T(128)}) while((s32[]{:T(128)}, f32[256,256]{1,0:T(8,128)S(1)}, s32[2,2]{1,0:T(2,128)S(1)}, f32[2,128,128]{2,1,0:T(8,128)S(1)}, s32[]{:T(128)}) %tuple.33), condition=%wide.while_cond.clone, body=%wide.while_body.clone.sunk | while | flops 2 | bytes 131189 | solution.py:595
  291.9 0.6 fusion.22
  292.5 1.4 bitcast_dynamic-update-slice_fusion.2
  293.9 0.6 fusion.22
  294.5 1.4 bitcast_dynamic-update-slice_fusion.2
  295.9 19.7 %custom-call.17 = f32[2,128,128]{1,2,0:T(8,128)S(1)} custom-call(f32[2,128,128]{2,1,0:T(8,128)S(1)} %get-tuple-element.24), custom_call_target="InvertDiagBlocksLowerTriangular" | custom-call | tf_op jit(solution)/shard_map/jit(_solve_triangular)/triangular_solve | solution.py:595
  315.6 0.3 fusion.4
  315.9 0.3 convolution_subtract_fusion.1
  316.2 0.3 fusion.10
  316.6 0.3 fusion.2
  316.9 0.4 convolution_subtract_fusion
  317.3 0.3 fusion.9
  317.6 0.7 pad_maximum_fusion
  318.3 0.0 copy-done
  318.3 0.6 copy.21
  (11 shorter events, 0.2 us)
Async XLA Ops:
  0.6 251.8 %copy-start.1 = (f32[2]{0:T(128)S(1)}, f32[2]{0:T(128)}, u32[]{:S(2)}) copy-start(f32[2]{0:T(128)} %bounds.1) | copy-start | bytes 28
  250.2 68.1 %copy-start = (f32[90,256]{1,0:T(8,128)S(1)}, f32[90,256]{1,0:T(8,128)}, u32[]{:S(2)}) copy-start(f32[90,256]{1,0:T(8,128)} %get-tuple-element.91) | copy-start | bytes 276484

commit v2 on v1

v2 whole, which is shorter than its diff:
```python
import jax
import jax.numpy as jnp
from jax import lax
from jax.experimental import pallas as pl
from jax.experimental.pallas import tpu as pltpu
from jax.sharding import PartitionSpec as P

MESH = pl.DeviceIdType.MESH
F32 = jnp.float32
BF16 = jnp.bfloat16
L = 128
TILE = 1440
PAD = 1536
PIECE = 96
OWN = 90
LEAD = 8

CHAIN = dict(
    raw0=((2, 4, 2, PIECE, L), F32),
    panel0=((PAD, L), F32),
    panel_r=((2, 4, 2, PIECE, L), F32),
    panel_c=((4, 4, 2, 48, L), F32),
    panel_f=((4, 4, 2, 48, L), F32),
    part_c=((4, 4, 2, 48, L), F32),
    part_r=((2, 4, 2, PIECE, L), F32),
    vcat=((PAD, 2 * L), BF16),
    core_in=((4, 2, PIECE, L), F32),
    y_in=((6, 2, 2, 48, L), F32),
    y_sum=((4, 2, 48, L), F32),
    z_in=((3, 2, 48, L), F32),
    x_in=((6, PIECE, L), F32),
    x_sum=((2, PIECE, L), F32),
    h_in=((2, 2, PIECE, L), F32),
    z1=((2, 48, L), F32),
    z2=((2, PIECE, L), F32),
    z4=((2, 48, L), F32),
)
REDUCE = dict(
    a=((2, 4, 4, 8, 256), F32),
    total=((2, 4, 4, 8, 256), F32),
    core_in=((4, 4, 8, 256), F32),
    x_in=((3, 4, 8, 256), F32),
    y_in=((3, 8, 256), F32),
    z_in=((8, 8, 256), F32),
)
SHARED = dict(
    stage=((TILE, TILE), F32),
    strip=((128, PAD), F32),
    mat_h=((PAD, PAD), BF16),
    mat_l=((PAD, PAD), BF16),
    tra_h=((PAD, PAD), BF16),
    tra_l=((PAD, PAD), BF16),
    own4=((128, 256), F32),
    ft_h=((256, PAD), BF16),
    ft_l=((256, PAD), BF16),
    img_h=((PAD, 256), BF16),
    img_l=((PAD, 256), BF16),
    work=((256, 512), F32),
    done=((256, 512), F32),
)
AT_START, AT_ROW, AT_ROWG, AT_COL, AT_COLG, AT_TURN, AT_LAST, CHAIN_SEMS = 0, 11, 20, 29, 39, 49, 50, 59
REDUCE_SEMS = 21


def split(value):
    high = value.astype(BF16)
    return high, (value - high.astype(F32)).astype(BF16)


def together(*tasks):
    tasks = list(tasks)
    while tasks:
        tasks = [t for t in tasks if next(t, "end") != "end"]
        if tasks:
            yield


def run(*tasks):
    for _ in together(*tasks):
        pass


class Kernel:
    def __init__(self):
        r, c = lax.axis_index("row"), lax.axis_index("col")
        self.r, self.c = r, c
        self.y, self.z = r // 4, r % 4
        self.zh, self.x, self.core = c // 8, (c // 2) % 4, c % 2
        self.pos = self.core * 8 + self.x * 2 + self.zh

    def yn(self, d):
        return ((self.y + d) % 4) * 4 + self.z, self.c

    def zn(self, d):
        return self.y * 4 + (self.z + d) % 4, self.c

    def xn(self, d):
        return self.r, self.zh * 8 + ((self.x + d) % 4) * 2 + self.core

    def zall(self, d):
        at = (self.zh * 4 + self.z + d) % 8
        return self.y * 4 + at % 4, (at // 4) * 8 + self.x * 2 + self.core

    def hn(self):
        return self.r, (1 - self.zh) * 8 + self.x * 2 + self.core

    def cn(self):
        return self.r, self.zh * 8 + self.x * 2 + 1 - self.core

    def turn_to(self):
        return self.pos, self.r

    def turn_from(self):
        r = self.r
        return self.c, (r % 2) * 8 + ((r // 2) % 4) * 2 + r // 8


class Link:
    def __init__(self, send, recv):
        self.send, self.recv, self.open = send, recv, []

    def put(self, src, dst, k, device):
        copy = pltpu.make_async_remote_copy(
            src_ref=src, dst_ref=dst, send_sem=self.send.at[k], recv_sem=self.recv.at[k], device_id=device, device_id_type=MESH
        )
        copy.start()
        self.open.append(copy)

    def got(self, dst, k, device):
        pltpu.make_async_remote_copy(
            src_ref=dst, dst_ref=dst, send_sem=self.send.at[k], recv_sem=self.recv.at[k], device_id=device, device_id_type=MESH
        ).wait_recv()

    def flush(self):
        for copy in self.open:
            copy.wait_send()
        self.open = []


def ring_sum(link, k, i, near, half, box, out, ready, slow):
    a, b, d = (i + 1) % 4, (i + 3) % 4, (i + 2) % 4
    ready(d)
    link.put(half(d, 0), box.at[0], k, near(1))
    link.put(half(d, 1), box.at[1], k + 1, near(3))
    if slow:
        yield
    ready(a)
    link.put(half(a, 1), box.at[2], k + 2, near(1))
    if slow:
        yield
    ready(b)
    link.put(half(b, 0), box.at[3], k + 3, near(3))
    if slow:
        yield
    ready(i)
    yield
    link.got(box.at[0], k, near(3))
    half(a, 0)[...] += box[0]
    link.put(half(a, 0), box.at[4], k + 4, near(1))
    link.got(box.at[1], k + 1, near(1))
    half(b, 1)[...] += box[1]
    link.put(half(b, 1), box.at[5], k + 5, near(3))
    yield
    link.got(box.at[2], k + 2, near(3))
    link.got(box.at[3], k + 3, near(1))
    link.got(box.at[4], k + 4, near(3))
    link.got(box.at[5], k + 5, near(1))
    out(0, half(i, 0)[...] + box[4] + box[3])
    out(1, half(i, 1)[...] + box[2] + box[5])


def gather_start(me, link, k, panel):
    own = panel.at[me.core, me.x, me.zh]
    link.put(own, own, k, me.hn())
    yield
    link.got(panel.at[me.core, me.x, 1 - me.zh], k, me.hn())
    yield from gather_col(me, link, k + 1, panel)


def gather_col(me, link, k, panel):
    core, x = me.core, me.x
    a, b, d = (x + 1) % 4, (x + 3) % 4, (x + 2) % 4
    other = 1 - core

    def put(ref, j, device):
        link.put(ref, ref, k + j, device)

    put(panel.at[core, x, 0], 0, me.xn(1))
    put(panel.at[core, x, 1], 1, me.xn(3))
    put(panel.at[core, x, 1], 2, me.xn(1))
    put(panel.at[core, x, 0], 3, me.xn(3))
    put(panel.at[core, x], 6, me.cn())
    yield
    link.got(panel.at[core, b, 0], k, me.xn(3))
    put(panel.at[core, b, 0], 4, me.xn(1))
    link.got(panel.at[core, a, 1], k + 1, me.xn(1))
    put(panel.at[core, a, 1], 5, me.xn(3))
    yield
    link.got(panel.at[core, b, 1], k + 2, me.xn(3))
    put(panel.at[core, b], 7, me.cn())
    link.got(panel.at[core, a, 0], k + 3, me.xn(1))
    put(panel.at[core, a], 8, me.cn())
    link.got(panel.at[core, d, 0], k + 4, me.xn(3))
    link.got(panel.at[core, d, 1], k + 5, me.xn(1))
    put(panel.at[core, d], 9, me.cn())
    yield
    link.got(panel.at[other, x], k + 6, me.cn())
    link.got(panel.at[other, b], k + 7, me.cn())
    link.got(panel.at[other, a], k + 8, me.cn())
    link.got(panel.at[other, d], k + 9, me.cn())


def gather_row(me, link, k, panel):
    y, z = me.y, me.z
    ya, yb, yd = (y + 1) % 4, (y + 3) % 4, (y + 2) % 4

    def put(ref, j, device):
        link.put(ref, ref, k + j, device)

    for d in (1, 2, 3):
        put(panel.at[y, z], d - 1, me.zn(d))
    yield
    for d in (1, 2, 3):
        link.got(panel.at[y, (z + 4 - d) % 4], k + d - 1, me.zn(4 - d))
    low, high = pl.ds(0, 2), pl.ds(2, 2)
    put(panel.at[y, low], 3, me.yn(1))
    put(panel.at[y, high], 4, me.yn(3))
    put(panel.at[y, high], 5, me.yn(1))
    put(panel.at[y, low], 6, me.yn(3))
    yield
    link.got(panel.at[yb, low], k + 3, me.yn(3))
    put(panel.at[yb, low], 7, me.yn(1))
    link.got(panel.at[ya, high], k + 4, me.yn(1))
    put(panel.at[ya, high], 8, me.yn(3))
    yield
    link.got(panel.at[yb, high], k + 5, me.yn(3))
    link.got(panel.at[ya, low], k + 6, me.yn(1))
    link.got(panel.at[yd, low], k + 7, me.yn(3))
    link.got(panel.at[yd, high], k + 8, me.yn(1))


def split_row_panel(panel, vcat):
    @pl.loop(0, 8)
    def _(i):
        high, low = split(panel[i // 4, i % 4].reshape(2 * PIECE, L))
        rows = pl.ds(pl.multiple_of(i * 192, 192), 192)
        vcat[rows, :L] = high
        vcat[rows, L:] = low


def split_col_panel(panel, vcat):
    @pl.loop(0, 4)
    def _(i):
        high, low = split(panel[i].reshape(384, L))
        rows = pl.ds(pl.multiple_of(i * 384, 384), 384)
        vcat[rows, :L] = high
        vcat[rows, L:] = low


def product(high, low, vcat, chunk):
    rows = pl.ds(pl.multiple_of(chunk * 384, 384), 384)
    wide = jnp.dot(high[rows, :], vcat[...], preferred_element_type=F32)
    rest = jnp.dot(low[rows, :], vcat[:, :L], preferred_element_type=F32)
    return wide[:, :L] + (wide[:, L:] + rest)


def odd_step(me, link, s, b, scale, previous, save):
    split_row_panel(b["panel_r"], b["vcat"]) if previous is not None else None
    part, y_sum, panel = b["part_c"], b["y_sum"], b["panel_c"]
    y, z = me.y, me.z

    def ready(j):
        part[j] = product(s["tra_h"], s["tra_l"], b["vcat"], j).reshape(4, 2, 48, L)

    def out_y(h, value):
        y_sum[pl.ds(2 * h, 2)] = value

    yield from ring_sum(link, AT_ROW, y, me.yn, lambda j, h: part.at[j, pl.ds(2 * h, 2)], b["y_in"], out_y, ready, True)
    box, k = b["z_in"], AT_ROW + 6
    for d in (1, 2, 3):
        link.put(y_sum.at[(z + d) % 4], box.at[d - 1], k + d - 1, me.zn(d))
    yield
    for d in (1, 2, 3):
        link.got(box.at[d - 1], k + d - 1, me.zn(4 - d))
    value = ((y_sum[z] + box[0]) + (box[1] + box[2])) * scale
    if previous is not None:
        value = value - previous[...]
    panel[y, z] = value
    if save is not None:
        save[...] = value
    yield from gather_row(me, link, AT_ROWG, panel)
    link.flush()


def even_sum(me, link, s, b, step, scale, previous, store):
    split_col_panel(b["panel_c"], b["vcat"])
    part, box = b["part_r"], b["core_in"]
    core, x = me.core, me.x
    other, first = 1 - core, 1 - x // 2
    k = AT_COL

    def compute(half, pair):
        value = product(s["mat_h"], s["mat_l"], b["vcat"], half * 2 + pair)
        part[half, pl.ds(2 * pair, 2)] = value.reshape(2, 2, PIECE, L)

    compute(other, first)
    link.put(part.at[other, pl.ds(2 * first, 2)], box.at[pl.ds(2 * first, 2)], k, me.cn())
    last = 1 - first
    yield
    compute(other, last)
    link.put(part.at[other, pl.ds(2 * last, 2)], box.at[pl.ds(2 * last, 2)], k + 1, me.cn())
    yield
    compute(core, first)
    yield
    compute(core, last)
    yield
    turn = []

    def ready(j):
        if len(turn) == 0:
            link.got(box.at[pl.ds(2 * first, 2)], k, me.cn())
        if len(turn) == 1:
            link.got(box.at[pl.ds(2 * last, 2)], k + 1, me.cn())
        turn.append(j)
        part[core, j] += box[j]

    x_sum = b["x_sum"]

    def out_x(h, value):
        x_sum[h] = value

    yield from ring_sum(link, k + 2, x, me.xn, lambda j, h: part.at[core, j, h], b["x_in"], out_x, ready, False)
    link.put(x_sum, b["h_in"].at[step], k + 8 + step, me.hn())
    yield
    link.got(b["h_in"].at[step], k + 8 + step, me.hn())
    store((x_sum[...] + b["h_in"][step]) * scale - previous())


def first_gather(me, link, b):
    yield from gather_start(me, link, AT_START, b["raw0"])
    panel0 = b["panel0"]
    panel0[TILE:, :] = jnp.zeros((PAD - TILE, L), F32)
    for c in range(16):
        panel0[c * OWN : (c + 1) * OWN, :] = b["raw0"][c % 2, (c // 2) % 4, c // 8, :OWN, :]

    @pl.loop(0, 4)
    def _(i):
        rows = pl.ds(pl.multiple_of(i * 384, 384), 384)
        high, low = split(panel0[rows, :])
        b["vcat"][rows, :L] = high
        b["vcat"][rows, L:] = low

    link.flush()


def chain(me, link, s, b, h, half_width, alone, reached):
    one, two = 1.0 / half_width, 2.0 / half_width
    yield from odd_step(me, link, s, b, one, None, b["z1"])
    panel0, z2, panel_r = b["panel0"], b["z2"], b["panel_r"]

    def store2(value):
        z2[...] = value
        panel_r[me.core, me.x] = value

    rows = pl.ds(pl.multiple_of((me.core * 4 + me.x) * 192, 192), 192)
    yield from even_sum(me, link, s, b, 0, two, lambda: panel0[rows, :].reshape(2, PIECE, L), store2)
    yield from gather_col(me, link, AT_COLG, panel_r)
    link.flush()
    yield from odd_step(me, link, s, b, two, b["z1"], None)

    def store4(value):
        panel_r[me.core, me.x] = value

    yield from even_sum(me, link, s, b, 1, two, lambda: z2[...], store4)
    link.flush()
    b["z4"][...] = panel_r[me.core, me.x, me.zh].reshape(2, 48, L)
    s["own4"][:PIECE, h * L : (h + 1) * L] = b["z4"][...].reshape(PIECE, L)
    reached.append("block")
    yield from together(gather_col(me, link, AT_COLG, panel_r), turned_gather(me, link, b, alone))
    link.flush()
    split_row_panel(panel_r, b["vcat"])
    for j in range(4):
        rows = slice(j * 384, (j + 1) * 384)
        high, low = split(product(s["tra_h"], s["tra_l"], b["vcat"], j))
        s["img_h"][rows, h * L : (h + 1) * L] = high
        s["img_l"][rows, h * L : (h + 1) * L] = low
        high, low = split(b["panel_f"][j].reshape(384, L).T)
        s["ft_h"][h * L : (h + 1) * L, rows] = high
        s["ft_l"][h * L : (h + 1) * L, rows] = low
        yield
    reached.append("image")


def turned_gather(me, link, b, alone):
    panel, z4 = b["panel_f"], b["z4"]
    row, col = me.turn_to()
    slot = panel.at[row // 4, row % 4]

    def copy():
        return pltpu.make_async_remote_copy(
            src_ref=z4,
            dst_ref=slot,
            send_sem=link.send.at[AT_TURN],
            recv_sem=link.recv.at[AT_TURN],
            device_id=(row, col),
            device_id_type=MESH,
        )

    @pl.when(jnp.logical_not(alone))
    def _():
        copy().start()

    @pl.when(alone)
    def _():
        panel[me.y, me.z] = z4[...]

    yield

    @pl.when(jnp.logical_not(alone))
    def _():
        link.got(panel.at[me.y, me.z], AT_TURN, me.turn_from())
        copy().wait_send()

    yield from gather_row(me, link, AT_LAST, panel)


def all_sum(me, link, b):
    a, total = b["a"], b["total"]
    y, z, x, core = me.y, me.z, me.x, me.core
    other = 1 - core
    link.put(a.at[other], b["core_in"], 0, me.cn())
    yield
    link.got(b["core_in"], 0, me.cn())
    a[core] += b["core_in"][...]
    for d in (1, 2, 3):
        link.put(a.at[core, (x + d) % 4], b["x_in"].at[d - 1], d, me.xn(d))
    yield
    for d in (1, 2, 3):
        link.got(b["x_in"].at[d - 1], d, me.xn(4 - d))
    a[core, x] += (b["x_in"][0] + b["x_in"][1]) + b["x_in"][2]
    for d in (1, 2, 3):
        link.put(a.at[core, x, (y + d) % 4], b["y_in"].at[d - 1], 3 + d, me.yn(d))
    yield
    for d in (1, 2, 3):
        link.got(b["y_in"].at[d - 1], 3 + d, me.yn(4 - d))
    at = me.zh * 4 + z
    box = b["z_in"]
    box[at] = a[core, x, y] + ((b["y_in"][0] + b["y_in"][1]) + b["y_in"][2])
    for d in range(1, 8):
        link.put(box.at[at], box.at[at], 6 + d, me.zall(d))
    yield
    for d in range(1, 8):
        link.got(box.at[(at + 8 - d) % 8], 6 + d, me.zall(8 - d))
    total[core, x, y] = ((box[0] + box[1]) + (box[2] + box[3])) + ((box[4] + box[5]) + (box[6] + box[7]))
    for d in (1, 2, 3):
        link.put(total.at[core, x, y], total.at[core, x, y], 13 + d, me.yn(d))
    yield
    for d in (1, 2, 3):
        link.got(total.at[core, x, (y + 4 - d) % 4], 13 + d, me.yn(4 - d))
    for d in (1, 2, 3):
        link.put(total.at[core, x], total.at[core, x], 16 + d, me.xn(d))
    yield
    for d in (1, 2, 3):
        link.got(total.at[core, (x + 4 - d) % 4], 16 + d, me.xn(4 - d))
    link.put(total.at[core], total.at[core], 20, me.cn())
    yield
    link.got(total.at[other], 20, me.cn())
    link.flush()


BLOCK = 64
GROUPS = BLOCK // 8


def eliminate(groups, turn):
    row = lax.broadcasted_iota(jnp.int32, (8, 128), 0)
    wide = (8, 128)

    def sub(value, j):
        return jnp.broadcast_to(value[j : j + 1, :], wide)

    for j in range(0, 8, 2):
        col0 = [jnp.broadcast_to(g[:, j : j + 1], wide) for g in groups]
        col1 = [jnp.broadcast_to(g[:, j + 1 : j + 2], wide) for g in groups]
        inv0 = 1.0 / sub(col0[0], j)
        lower = sub(col0[0], j + 1) * inv0
        upper = sub(col1[0], j)
        inv1 = 1.0 / (sub(col1[0], j + 1) - lower * upper)
        row0 = sub(groups[0], j)
        row1 = sub(groups[0], j + 1) - lower * row0
        for g in range(GROUPS):
            mul0 = col0[g] * inv0
            mul1 = (col1[g] - mul0 * upper) * inv1
            if g == 0:
                mul0 = jnp.where(row > j, mul0, 0.0)
                mul1 = jnp.where(row > j + 1, mul1, 0.0)
            else:
                left = turn + g < GROUPS
                mul0 = jnp.where(left, mul0, 0.0)
                mul1 = jnp.where(left, mul1, 0.0)
            groups[g] = groups[g] - mul0 * row0 - mul1 * row1
    return [pltpu.roll(g, 120, 1) for g in groups[1:] + groups[:1]]


def exact(p, q, dims):
    return lax.dot_general(p, q, (dims, ((), ())), precision=lax.Precision.HIGHEST, preferred_element_type=F32)


def invert_factor(s, gram):
    work, done = s["work"], s["done"]
    row = lax.broadcasted_iota(jnp.int32, (256, 256), 0)
    col = lax.broadcasted_iota(jnp.int32, (256, 256), 1)
    work[:, :256] = gram
    work[:, 256:] = jnp.where(row == col, 1.0, 0.0)
    small_row = lax.broadcasted_iota(jnp.int32, (BLOCK, 128), 0)
    small_col = lax.broadcasted_iota(jnp.int32, (BLOCK, 128), 1)
    for b in range(256 // BLOCK):
        rows = slice(b * BLOCK, (b + 1) * BLOCK)
        lanes = b * BLOCK // 128 * 128
        block = work[rows, lanes : lanes + 128]
        if b % 2:
            block = pltpu.roll(block, 64, 1)
        block = jnp.where(small_col < BLOCK, block, jnp.where(small_col == small_row + BLOCK, 1.0, 0.0))
        groups = tuple(block[8 * g : 8 * g + 8] for g in range(GROUPS))
        for half in range(2):
            at = half * GROUPS // 2
            groups = lax.fori_loop(at, at + GROUPS // 2, lambda i, gs: tuple(eliminate(list(gs), i)), groups)
            yield
        block = jnp.concatenate(groups, axis=0)
        pivot = jnp.sum(jnp.where(small_col == small_row + BLOCK, block, 0.0), axis=1, keepdims=True)
        root = lax.rsqrt(pivot)
        root = root * (1.5 - 0.5 * pivot * root * root)
        inverse = (block * root)[:, :BLOCK]
        mine = exact(inverse, work[rows, :], ((1,), (0,)))
        done[rows, :] = mine
        if b < 256 // BLOCK - 1:
            after = exact(mine[:, :256], mine, ((0,), (0,)))
            work[(b + 1) * BLOCK :, :] -= after[(b + 1) * BLOCK :, :]
        yield


def gram_task(me, link, s, b, reached):
    while reached.count("block") < 2:
        yield
    high, low = split(s["own4"][...])
    dims = (((0,), (0,)), ((), ()))

    def pair(p, q):
        return lax.dot_general(p, q, dims, preferred_element_type=F32)

    part = pair(high, high) + (pair(high, low) + pair(low, high))
    b["a"][...] = part.reshape(2, 4, 4, 8, 256)
    yield from all_sum(me, link, b)
    yield from invert_factor(s, b["total"][...].reshape(256, 256))


def projected_task(me, link, s, b, reached):
    while reached.count("image") < 2:
        yield

    def inner(p, q):
        return jnp.dot(p[...], q[...], preferred_element_type=F32)

    part = inner(s["ft_h"], s["img_h"]) + (inner(s["ft_h"], s["img_l"]) + inner(s["ft_l"], s["img_h"]))
    b["a"][...] = part.reshape(2, 4, 4, 8, 256)
    yield from all_sum(me, link, b)


def body_kernel(lap, block, bounds, filtered, rayleigh, *scratch):
    names = list(SHARED), list(CHAIN), list(CHAIN), list(REDUCE), list(REDUCE)
    groups, at = [], 0
    for group in names:
        groups.append(dict(zip(group, scratch[at : at + len(group)])))
        at += len(group)
    s, *chains, red_g, red_p = groups
    lap_sem, *sems = scratch[at:]
    links = [Link(sems[2 * i], sems[2 * i + 1]) for i in range(4)]
    me = Kernel()
    to_row, to_col = me.turn_to()
    alone = jnp.logical_and(to_row == me.r, to_col == me.c)

    load = pltpu.make_async_copy(lap, s["stage"], lap_sem)
    load.start()
    for h, b in enumerate(chains):
        own = b["raw0"].at[me.core, me.x, me.zh]
        own[OWN - 2 :, :] = jnp.zeros((PIECE - OWN + 2, L), F32)
        own[:OWN, :] = block[:, h * L : (h + 1) * L]

    barrier = pltpu.get_barrier_semaphore()
    near = [f(d) for f in (me.yn, me.xn) for d in (1, 2, 3)] + [me.zall(d) for d in range(1, 8)] + [me.cn()]
    for device in near:
        pl.semaphore_signal(barrier, inc=1, device_id=device, device_id_type=MESH)

    @pl.when(jnp.logical_not(alone))
    def _():
        pl.semaphore_signal(barrier, inc=1, device_id=me.turn_to(), device_id_type=MESH)
        pl.semaphore_signal(barrier, inc=1, device_id=me.turn_from(), device_id_type=MESH)

    pl.semaphore_wait(barrier, jnp.where(alone, len(near), len(near) + 2))

    center = (bounds[1] + bounds[0]) * 0.5
    half_width = (bounds[1] - bounds[0]) * 0.5

    def prepare():
        load.wait()
        shift = jnp.where(me.r == me.c, center, 0.0)
        strip = s["strip"]
        strip[...] = jnp.zeros_like(strip)

        def strip_of(start, count):
            value = s["stage"][pl.ds(start, count), :]
            row = start + lax.broadcasted_iota(jnp.int32, (count, TILE), 0)
            col = lax.broadcasted_iota(jnp.int32, (count, TILE), 1)
            strip[:count, :TILE] = value - jnp.where(row == col, shift, 0.0)

        def spread(start):
            whole = strip[...]
            high, low = split(whole)
            s["mat_h"][pl.ds(start, 128), :] = high
            s["mat_l"][pl.ds(start, 128), :] = low
            high, low = split(whole.T)
            s["tra_h"][:, pl.ds(start, 128)] = high
            s["tra_l"][:, pl.ds(start, 128)] = low

        for at in (0, 3, 6, 9):

            @pl.loop(at, min(at + 3, TILE // 128))
            def _(i):
                start = pl.multiple_of(i * 128, 128)
                strip_of(start, 128)
                spread(start)

            yield

        strip[...] = jnp.zeros_like(strip)
        strip_of(TILE // 128 * 128, TILE % 128)
        spread(TILE // 128 * 128)

    s["own4"][PIECE:, :] = jnp.zeros((128 - PIECE, 256), F32)
    reached = []
    one, two = (chain(me, links[h], s, chains[h], h, half_width, alone, reached) for h in (0, 1))
    start = [first_gather(me, links[h], chains[h]) for h in (0, 1)]
    run(start[0], prepare())
    late = together(start[1])
    for _ in range(LEAD):
        next(one)
        next(late, None)

    def second():
        yield from late
        yield from two

    run(one, second(), gram_task(me, links[2], s, red_g, reached), projected_task(me, links[3], s, red_p, reached))
    for c in range(16):

        @pl.when(me.c == c)
        def _(c=c):
            for h, b in enumerate(chains):
                row = 0
                while row < OWN:
                    at = c * OWN + row
                    p, inside = at // PIECE, at % PIECE
                    count = min(PIECE - inside, OWN - row)
                    filtered[row : row + count, h * L : (h + 1) * L] = b["panel_r"][p // 8, (p // 2) % 4, p % 2, inside : inside + count, :]
                    row += count

    projected = red_p["total"][...].reshape(256, 256) + center * red_g["total"][...].reshape(256, 256)
    projected = (projected + projected.T) * 0.5
    inverse = s["done"][:, 256:]
    rayleigh[...] = exact(exact(inverse, projected, ((1,), (0,))), inverse, ((1,), (1,)))


def body(laplacian, block, bounds):
    vmem = pl.BlockSpec(memory_space=pltpu.VMEM)
    scratch = [pltpu.VMEM(shape, kind) for group in (SHARED, CHAIN, CHAIN, REDUCE, REDUCE) for shape, kind in group.values()]
    scratch.append(pltpu.SemaphoreType.DMA)
    for count in (CHAIN_SEMS, CHAIN_SEMS, REDUCE_SEMS, REDUCE_SEMS):
        scratch += [pltpu.SemaphoreType.DMA((count,)), pltpu.SemaphoreType.DMA((count,))]
    return pl.pallas_call(
        body_kernel,
        out_shape=(jax.ShapeDtypeStruct(block.shape, F32), jax.ShapeDtypeStruct((256, 256), F32)),
        in_specs=[pl.BlockSpec(memory_space=pl.ANY), vmem, pl.BlockSpec(memory_space=pltpu.SMEM)],
        out_specs=(vmem, vmem),
        scratch_shapes=scratch,
        compiler_params=pltpu.CompilerParams(collective_id=0, has_side_effects=True, vmem_limit_bytes=62 * 1024 * 1024),
        name="filter",
    )(laplacian, block, bounds)


def solution(mesh):
    placed = (P("row", "col"), P(("row", "col"), None), P())
    return jax.shard_map(
        body, mesh=mesh, in_specs=placed, out_specs=(P(("row", "col"), None), P()), check_vma=False
    )
```

time: 319 us -> 269 us (0.84)
  other arithmetic: 55.8 us -> 0 us
  Pallas kernels: 250 us -> 265 us
  local copies, waits for them, and re-layouts: 7.7 us -> 3.21 us
    another operation x11 -> x0, other arithmetic: 54.7 us -> none  [the longest x6 34 us: body(): factor = jnp.linalg.cholesky(gram)]
    pallas_call x1, Pallas kernels: 250 us -> 265 us  [body(): pl.pallas_call(body_kernel, out_shape=(jax.ShapeDtypeStruct(block.shape,...]
    another operation x9 -> x0, local copies, waits for them, and re-layouts: 4.16 us -> none  [the longest x7 4.13 us: body(): jax.scipy.linalg.solve_triangular(factor, first_solve.T, lower=True)]
where the time goes in v2:
time: 269 us
  Pallas kernels  265 us (99%)
  local copies, waits for them, and re-layouts  3.21 us (1%)
    pallas_call x1, Pallas kernels, body(): pl.pallas_call(body_kernel, out_shape=(jax.ShapeDtypeStruct(block.shape,...  265 us

profile of v2, /device:TPU:1, one launch (start us, length us, event | category | flops | bytes accessed | tf_op | source)
XLA Modules:
  0.0 269.2 jit_solution(17852627581216093794)
XLA Ops:
  0.6 265.4 %filter.1 = (f32[90,256]{1,0:T(8,128)}, f32[256,256]{1,0:T(8,128)}) custom-call(f32[1440,1440]{1,0:T(8,128)} %lap.1, f32[90,256]{1,0:T(8,128)} %block.1, f32[2]{0:T(128)} %bounds.1), custom_call_target="tpu_custom_call" | custom-call | tf_op jit(solution)/shard_map/filter/pallas_call | solution.py:679
  266.0 1.5 copy.7
  267.6 1.7 copy.8

commit v3 on v2

--- a/solution.py
+++ b/solution.py
@@ -13,7 +13,6 @@
 PAD = 1536
 PIECE = 96
 OWN = 90
-LEAD = 8
 
 CHAIN = dict(
     raw0=((2, 4, 2, PIECE, L), F32),
@@ -35,14 +34,19 @@
     z2=((2, PIECE, L), F32),
     z4=((2, 48, L), F32),
 )
-REDUCE = dict(
-    a=((2, 4, 4, 8, 256), F32),
-    total=((2, 4, 4, 8, 256), F32),
-    core_in=((4, 4, 8, 256), F32),
-    x_in=((3, 4, 8, 256), F32),
-    y_in=((3, 8, 256), F32),
-    z_in=((8, 8, 256), F32),
-)
+def reduce_of(piece):
+    cut = (4, *piece) if piece[0] == 8 else piece
+    return dict(
+        a=((2, 4, *cut), F32),
+        total=((2, 4, *cut), F32),
+        core_in=((4, *cut), F32),
+        x_in=((3, *cut), F32),
+        y_in=((4, *piece), F32),
+        z_in=((8, *piece), F32),
+    )
+
+
+REDUCES = reduce_of((16, L)), reduce_of((8, L)), reduce_of((8, 256))
 SHARED = dict(
     stage=((TILE, TILE), F32),
     strip=((128, PAD), F32),
@@ -55,8 +59,11 @@
     ft_l=((256, PAD), BF16),
     img_h=((PAD, 256), BF16),
     img_l=((PAD, 256), BF16),
-    work=((256, 512), F32),
-    done=((256, 512), F32),
+    work=((L, 256), F32),
+    done0=((L, 256), F32),
+    done1=((L, 256), F32),
+    inverse=((256, 256), F32),
+    gram=((256, 256), F32),
 )
 AT_START, AT_ROW, AT_ROWG, AT_COL, AT_COLG, AT_TURN, AT_LAST, CHAIN_SEMS = 0, 11, 20, 29, 39, 49, 50, 59
 REDUCE_SEMS = 21
@@ -137,21 +144,15 @@
         self.open = []
 
 
-def ring_sum(link, k, i, near, half, box, out, ready, slow):
+def ring_sum(link, k, i, near, half, box, out, ready):
     a, b, d = (i + 1) % 4, (i + 3) % 4, (i + 2) % 4
     ready(d)
     link.put(half(d, 0), box.at[0], k, near(1))
     link.put(half(d, 1), box.at[1], k + 1, near(3))
-    if slow:
-        yield
     ready(a)
     link.put(half(a, 1), box.at[2], k + 2, near(1))
-    if slow:
-        yield
     ready(b)
     link.put(half(b, 0), box.at[3], k + 3, near(3))
-    if slow:
-        yield
     ready(i)
     yield
     link.got(box.at[0], k, near(3))
@@ -275,7 +276,7 @@
     def out_y(h, value):
         y_sum[pl.ds(2 * h, 2)] = value
 
-    yield from ring_sum(link, AT_ROW, y, me.yn, lambda j, h: part.at[j, pl.ds(2 * h, 2)], b["y_in"], out_y, ready, True)
+    yield from ring_sum(link, AT_ROW, y, me.yn, lambda j, h: part.at[j, pl.ds(2 * h, 2)], b["y_in"], out_y, ready)
     box, k = b["z_in"], AT_ROW + 6
     for d in (1, 2, 3):
         link.put(y_sum.at[(z + d) % 4], box.at[d - 1], k + d - 1, me.zn(d))
@@ -306,12 +307,9 @@
     compute(other, first)
     link.put(part.at[other, pl.ds(2 * first, 2)], box.at[pl.ds(2 * first, 2)], k, me.cn())
     last = 1 - first
-    yield
     compute(other, last)
     link.put(part.at[other, pl.ds(2 * last, 2)], box.at[pl.ds(2 * last, 2)], k + 1, me.cn())
-    yield
     compute(core, first)
-    yield
     compute(core, last)
     yield
     turn = []
@@ -329,7 +327,7 @@
     def out_x(h, value):
         x_sum[h] = value
 
-    yield from ring_sum(link, k + 2, x, me.xn, lambda j, h: part.at[core, j, h], b["x_in"], out_x, ready, False)
+    yield from ring_sum(link, k + 2, x, me.xn, lambda j, h: part.at[core, j, h], b["x_in"], out_x, ready)
     link.put(x_sum, b["h_in"].at[step], k + 8 + step, me.hn())
     yield
     link.got(b["h_in"].at[step], k + 8 + step, me.hn())
@@ -376,18 +374,24 @@
     b["z4"][...] = panel_r[me.core, me.x, me.zh].reshape(2, 48, L)
     s["own4"][:PIECE, h * L : (h + 1) * L] = b["z4"][...].reshape(PIECE, L)
     reached.append("block")
-    yield from together(gather_col(me, link, AT_COLG, panel_r), turned_gather(me, link, b, alone))
+
+    def image():
+        yield from gather_col(me, link, AT_COLG, panel_r)
+        split_row_panel(panel_r, b["vcat"])
+        for j in range(4):
+            high, low = split(product(s["tra_h"], s["tra_l"], b["vcat"], j))
+            s["img_h"][j * 384 : (j + 1) * 384, h * L : (h + 1) * L] = high
+            s["img_l"][j * 384 : (j + 1) * 384, h * L : (h + 1) * L] = low
+
+    def rows_across():
+        yield from turned_gather(me, link, b, alone)
+        for j in range(4):
+            high, low = split(b["panel_f"][j].reshape(384, L).T)
+            s["ft_h"][h * L : (h + 1) * L, j * 384 : (j + 1) * 384] = high
+            s["ft_l"][h * L : (h + 1) * L, j * 384 : (j + 1) * 384] = low
+
+    yield from together(image(), rows_across())
     link.flush()
-    split_row_panel(panel_r, b["vcat"])
-    for j in range(4):
-        rows = slice(j * 384, (j + 1) * 384)
-        high, low = split(product(s["tra_h"], s["tra_l"], b["vcat"], j))
-        s["img_h"][rows, h * L : (h + 1) * L] = high
-        s["img_l"][rows, h * L : (h + 1) * L] = low
-        high, low = split(b["panel_f"][j].reshape(384, L).T)
-        s["ft_h"][h * L : (h + 1) * L, rows] = high
-        s["ft_l"][h * L : (h + 1) * L, rows] = low
-        yield
     reached.append("image")
 
 
@@ -428,6 +432,7 @@
     a, total = b["a"], b["total"]
     y, z, x, core = me.y, me.z, me.x, me.core
     other = 1 - core
+    whole = len(a.shape) == 4
     link.put(a.at[other], b["core_in"], 0, me.cn())
     yield
     link.got(b["core_in"], 0, me.cn())
@@ -437,26 +442,37 @@
     yield
     for d in (1, 2, 3):
         link.got(b["x_in"].at[d - 1], d, me.xn(4 - d))
-    a[core, x] += (b["x_in"][0] + b["x_in"][1]) + b["x_in"][2]
-    for d in (1, 2, 3):
-        link.put(a.at[core, x, (y + d) % 4], b["y_in"].at[d - 1], 3 + d, me.yn(d))
-    yield
-    for d in (1, 2, 3):
-        link.got(b["y_in"].at[d - 1], 3 + d, me.yn(4 - d))
+    near = a[core, x] + ((b["x_in"][0] + b["x_in"][1]) + b["x_in"][2])
+    box = b["y_in"]
+    if whole:
+        box[y] = near
+    else:
+        a[core, x] = near
+        box[y] = a[core, x, y]
+    for d in (1, 2, 3):
+        place = (y + d) % 4
+        link.put(box.at[y] if whole else a.at[core, x, place], box.at[y], 3 + d, me.yn(d))
+    yield
+    for d in (1, 2, 3):
+        link.got(box.at[(y + 4 - d) % 4], 3 + d, me.yn(4 - d))
     at = me.zh * 4 + z
-    box = b["z_in"]
-    box[at] = a[core, x, y] + ((b["y_in"][0] + b["y_in"][1]) + b["y_in"][2])
+    near, box = (box[0] + box[1]) + (box[2] + box[3]), b["z_in"]
+    box[at] = near
     for d in range(1, 8):
         link.put(box.at[at], box.at[at], 6 + d, me.zall(d))
     yield
     for d in range(1, 8):
         link.got(box.at[(at + 8 - d) % 8], 6 + d, me.zall(8 - d))
-    total[core, x, y] = ((box[0] + box[1]) + (box[2] + box[3])) + ((box[4] + box[5]) + (box[6] + box[7]))
-    for d in (1, 2, 3):
-        link.put(total.at[core, x, y], total.at[core, x, y], 13 + d, me.yn(d))
-    yield
-    for d in (1, 2, 3):
-        link.got(total.at[core, x, (y + 4 - d) % 4], 13 + d, me.yn(4 - d))
+    near = ((box[0] + box[1]) + (box[2] + box[3])) + ((box[4] + box[5]) + (box[6] + box[7]))
+    if whole:
+        total[core, x] = near
+    else:
+        total[core, x, y] = near
+        for d in (1, 2, 3):
+            link.put(total.at[core, x, y], total.at[core, x, y], 13 + d, me.yn(d))
+        yield
+        for d in (1, 2, 3):
+            link.got(total.at[core, x, (y + 4 - d) % 4], 13 + d, me.yn(4 - d))
     for d in (1, 2, 3):
         link.put(total.at[core, x], total.at[core, x], 16 + d, me.xn(d))
     yield
@@ -506,52 +522,77 @@
     return lax.dot_general(p, q, (dims, ((), ())), precision=lax.Precision.HIGHEST, preferred_element_type=F32)
 
 
-def invert_factor(s, gram):
-    work, done = s["work"], s["done"]
-    row = lax.broadcasted_iota(jnp.int32, (256, 256), 0)
-    col = lax.broadcasted_iota(jnp.int32, (256, 256), 1)
-    work[:, :256] = gram
-    work[:, 256:] = jnp.where(row == col, 1.0, 0.0)
-    small_row = lax.broadcasted_iota(jnp.int32, (BLOCK, 128), 0)
-    small_col = lax.broadcasted_iota(jnp.int32, (BLOCK, 128), 1)
-    for b in range(256 // BLOCK):
+def invert_factor(work, done, gram):
+    row = lax.broadcasted_iota(jnp.int32, (L, L), 0)
+    col = lax.broadcasted_iota(jnp.int32, (L, L), 1)
+    work[:, :L] = gram
+    work[:, L:] = jnp.where(row == col, 1.0, 0.0)
+    row = lax.broadcasted_iota(jnp.int32, (BLOCK, L), 0)
+    col = lax.broadcasted_iota(jnp.int32, (BLOCK, L), 1)
+    for b in range(L // BLOCK):
         rows = slice(b * BLOCK, (b + 1) * BLOCK)
-        lanes = b * BLOCK // 128 * 128
-        block = work[rows, lanes : lanes + 128]
+        block = work[rows, :L]
         if b % 2:
             block = pltpu.roll(block, 64, 1)
-        block = jnp.where(small_col < BLOCK, block, jnp.where(small_col == small_row + BLOCK, 1.0, 0.0))
+        block = jnp.where(col < BLOCK, block, jnp.where(col == row + BLOCK, 1.0, 0.0))
         groups = tuple(block[8 * g : 8 * g + 8] for g in range(GROUPS))
         for half in range(2):
             at = half * GROUPS // 2
             groups = lax.fori_loop(at, at + GROUPS // 2, lambda i, gs: tuple(eliminate(list(gs), i)), groups)
             yield
         block = jnp.concatenate(groups, axis=0)
-        pivot = jnp.sum(jnp.where(small_col == small_row + BLOCK, block, 0.0), axis=1, keepdims=True)
+        pivot = jnp.sum(jnp.where(col == row + BLOCK, block, 0.0), axis=1, keepdims=True)
         root = lax.rsqrt(pivot)
         root = root * (1.5 - 0.5 * pivot * root * root)
         inverse = (block * root)[:, :BLOCK]
         mine = exact(inverse, work[rows, :], ((1,), (0,)))
         done[rows, :] = mine
-        if b < 256 // BLOCK - 1:
-            after = exact(mine[:, :256], mine, ((0,), (0,)))
+        if b < L // BLOCK - 1:
+            after = exact(mine[:, :L], mine, ((0,), (0,)))
             work[(b + 1) * BLOCK :, :] -= after[(b + 1) * BLOCK :, :]
+
+
+def inner_own(p, q):
+    dims = (((0,), (0,)), ((), ()))
+    (p_h, p_l), (q_h, q_l) = split(p), split(q)
+
+    def pair(u, v):
+        return lax.dot_general(u, v, dims, preferred_element_type=F32)
+
+    return pair(p_h, q_h) + (pair(p_h, q_l) + pair(p_l, q_h))
+
+
+def gram_first(me, link, s, b, reached):
+    while reached.count("block") < 1:
         yield
-
-
-def gram_task(me, link, s, b, reached):
+    own = s["own4"][:, :L]
+    b["a"][...] = inner_own(own, own).reshape(2, 4, 16, L)
+    yield from all_sum(me, link, b)
+    gram = b["total"][...].reshape(L, L)
+    s["gram"][:L, :L] = gram
+    yield from invert_factor(s["work"], s["done0"], gram)
+    s["inverse"][:L, :L] = s["done0"][:, L:]
+    s["inverse"][:L, L:] = jnp.zeros((L, L), F32)
+    reached.append("corner")
+
+
+def gram_second(me, link, s, b, reached):
     while reached.count("block") < 2:
         yield
-    high, low = split(s["own4"][...])
-    dims = (((0,), (0,)), ((), ()))
-
-    def pair(p, q):
-        return lax.dot_general(p, q, dims, preferred_element_type=F32)
-
-    part = pair(high, high) + (pair(high, low) + pair(low, high))
-    b["a"][...] = part.reshape(2, 4, 4, 8, 256)
+    b["a"][...] = inner_own(s["own4"][...], s["own4"][:, L:]).reshape(2, 4, 4, 8, L)
     yield from all_sum(me, link, b)
-    yield from invert_factor(s, b["total"][...].reshape(256, 256))
+    while reached.count("corner") < 1:
+        yield
+    cols = b["total"][...].reshape(256, L)
+    cross = cols[:L]
+    s["gram"][:, L:] = cols
+    s["gram"][L:, :L] = cross.T
+    first = s["inverse"][:L, :L]
+    upper = exact(first, cross, ((1,), (0,)))
+    yield from invert_factor(s["work"], s["done1"], cols[L:] - exact(upper, upper, ((0,), (0,))))
+    second = s["done1"][:, L:]
+    s["inverse"][L:, L:] = second
+    s["inverse"][L:, :L] = -exact(second, exact(upper, first, ((0,), (0,))), ((1,), (0,)))
 
 
 def projected_task(me, link, s, b, reached):
@@ -567,14 +608,14 @@
 
 
 def body_kernel(lap, block, bounds, filtered, rayleigh, *scratch):
-    names = list(SHARED), list(CHAIN), list(CHAIN), list(REDUCE), list(REDUCE)
+    names = [list(group) for group in (SHARED, CHAIN, CHAIN, *REDUCES)]
     groups, at = [], 0
     for group in names:
         groups.append(dict(zip(group, scratch[at : at + len(group)])))
         at += len(group)
-    s, *chains, red_g, red_p = groups
+    s, chains, reduces = groups[0], groups[1:3], groups[3:]
     lap_sem, *sems = scratch[at:]
-    links = [Link(sems[2 * i], sems[2 * i + 1]) for i in range(4)]
+    links = [Link(sems[2 * i], sems[2 * i + 1]) for i in range(5)]
     me = Kernel()
     to_row, to_col = me.turn_to()
     alone = jnp.logical_and(to_row == me.r, to_col == me.c)
@@ -640,17 +681,17 @@
     reached = []
     one, two = (chain(me, links[h], s, chains[h], h, half_width, alone, reached) for h in (0, 1))
     start = [first_gather(me, links[h], chains[h]) for h in (0, 1)]
+    late = together(start[1])
+    next(late)
     run(start[0], prepare())
-    late = together(start[1])
-    for _ in range(LEAD):
-        next(one)
-        next(late, None)
 
     def second():
         yield from late
         yield from two
 
-    run(one, second(), gram_task(me, links[2], s, red_g, reached), projected_task(me, links[3], s, red_p, reached))
+    corner = gram_first(me, links[2], s, reduces[0], reached)
+    rest = gram_second(me, links[3], s, reduces[1], reached)
+    run(one, second(), corner, rest, projected_task(me, links[4], s, reduces[2], reached), rest)
     for c in range(16):
 
         @pl.when(me.c == c)
@@ -664,17 +705,17 @@
                     filtered[row : row + count, h * L : (h + 1) * L] = b["panel_r"][p // 8, (p // 2) % 4, p % 2, inside : inside + count, :]
                     row += count
 
-    projected = red_p["total"][...].reshape(256, 256) + center * red_g["total"][...].reshape(256, 256)
-    projected = (projected + projected.T) * 0.5
-    inverse = s["done"][:, 256:]
+    projected = reduces[2]["total"][...].reshape(256, 256)
+    projected = (projected + projected.T) * 0.5 + center * s["gram"][...]
+    inverse = s["inverse"][...]
     rayleigh[...] = exact(exact(inverse, projected, ((1,), (0,))), inverse, ((1,), (1,)))
 
 
 def body(laplacian, block, bounds):
     vmem = pl.BlockSpec(memory_space=pltpu.VMEM)
-    scratch = [pltpu.VMEM(shape, kind) for group in (SHARED, CHAIN, CHAIN, REDUCE, REDUCE) for shape, kind in group.values()]
+    scratch = [pltpu.VMEM(shape, kind) for group in (SHARED, CHAIN, CHAIN, *REDUCES) for shape, kind in group.values()]
     scratch.append(pltpu.SemaphoreType.DMA)
-    for count in (CHAIN_SEMS, CHAIN_SEMS, REDUCE_SEMS, REDUCE_SEMS):
+    for count in (CHAIN_SEMS, CHAIN_SEMS, REDUCE_SEMS, REDUCE_SEMS, REDUCE_SEMS):
         scratch += [pltpu.SemaphoreType.DMA((count,)), pltpu.SemaphoreType.DMA((count,))]
     return pl.pallas_call(
         body_kernel,

time: 269 us -> 227 us (0.84)
  Pallas kernels: 265 us -> 223 us
    pallas_call x1, Pallas kernels: 265 us -> 223 us  [body(): pl.pallas_call(body_kernel, out_shape=(jax.ShapeDtypeStruct(block.shape,...]
where the time goes in v3:
time: 227 us
  Pallas kernels  223 us (98%)
  local copies, waits for them, and re-layouts  3.21 us (1%)
    pallas_call x1, Pallas kernels, body(): pl.pallas_call(body_kernel, out_shape=(jax.ShapeDtypeStruct(block.shape,...  223 us

profile of v3, /device:TPU:1, one launch (start us, length us, event | category | flops | bytes accessed | tf_op | source)
XLA Modules:
  0.0 226.6 jit_solution(13624865975341183080)
XLA Ops:
  0.6 222.8 %filter.1 = (f32[90,256]{1,0:T(8,128)}, f32[256,256]{1,0:T(8,128)}) custom-call(f32[1440,1440]{1,0:T(8,128)} %lap.1, f32[90,256]{1,0:T(8,128)} %block.1, f32[2]{0:T(128)} %bounds.1), custom_call_target="tpu_custom_call" | custom-call | tf_op jit(solution)/shard_map/filter/pallas_call | solution.py:720
  223.4 1.5 copy.7
  224.9 1.7 copy.8

commit v4 on v3

--- a/solution.py
+++ b/solution.py
@@ -632,12 +632,7 @@
     for device in near:
         pl.semaphore_signal(barrier, inc=1, device_id=device, device_id_type=MESH)
 
-    @pl.when(jnp.logical_not(alone))
-    def _():
-        pl.semaphore_signal(barrier, inc=1, device_id=me.turn_to(), device_id_type=MESH)
-        pl.semaphore_signal(barrier, inc=1, device_id=me.turn_from(), device_id_type=MESH)
-
-    pl.semaphore_wait(barrier, jnp.where(alone, len(near), len(near) + 2))
+    pl.semaphore_wait(barrier, len(near))
 
     center = (bounds[1] + bounds[0]) * 0.5
     half_width = (bounds[1] - bounds[0]) * 0.5

time: 227 us -> 226 us (level)
  no operation moved by 1% of the time
where the time goes in v4:
time: 226 us
  Pallas kernels  222 us (98%)
  local copies, waits for them, and re-layouts  3.21 us (1%)
    pallas_call x1, Pallas kernels, body(): pl.pallas_call(body_kernel, out_shape=(jax.ShapeDtypeStruct(block.shape,...  222 us

profile of v4, /device:TPU:1, one launch (start us, length us, event | category | flops | bytes accessed | tf_op | source)
XLA Modules:
  0.0 225.5 jit_solution(6489500318620501910)
XLA Ops:
  0.6 221.7 %filter.1 = (f32[90,256]{1,0:T(8,128)}, f32[256,256]{1,0:T(8,128)}) custom-call(f32[1440,1440]{1,0:T(8,128)} %lap.1, f32[90,256]{1,0:T(8,128)} %block.1, f32[2]{0:T(128)} %bounds.1), custom_call_target="tpu_custom_call" | custom-call | tf_op jit(solution)/shard_map/filter/pallas_call | solution.py:715
  222.3 1.5 copy.7
  223.8 1.7 copy.8
